TPU v7x, 256 devices: a whole 4x4x8 slice. The times are simulated.
256 devices in a mesh: tm: 16 (over z, core), panel: 16 (over y, x).
Axes of the slice: x: 4, y: 4, z: 8, core: 2. Of those that a mesh axis runs over, the one named last changes fastest.
Arguments:
- dynamics: bfloat16 [16, 1536, 1536], P('tm', 'panel'), may hold values from -1 to 1
- coupling: bfloat16 [16, 1536, 1536], P('tm', 'panel'), may hold values from -1 to 1
- cost_matrix: bfloat16 [16, 1536, 1536], P('tm', 'panel'), may hold values from -1 to 1
- band_offset: int32 [16, 12], P('tm'), may hold values from -1 to 0
- band_width: int32 [16, 12], P('tm'), may hold values from 2 to 3
Outputs:
- level_one: bfloat16 [16, 3, 1536, 1536], P('tm', None, 'panel')
- level_two: bfloat16 [16, 3, 1536, 1536], P('tm', None, 'panel')
All inputs are finite; a program needn't handle non-finite values.
Results may differ from a plain program's by a relative error of at most 0.012.
The roundings to bfloat16 on the way count: a program that leaves them out, or rounds other values in their place, can miss the bound.
Values may be sent and summed in bfloat16 or wider, within the bound.
A program may use at most 128 MiB of HBM per device.

v0:
```python
import jax
import jax.numpy as jnp
from jax import lax
from jax.sharding import PartitionSpec as P

BLOCK = 128
LEVELS = 2


def passed_along(value, axis, by):
    count = lax.axis_size(axis)
    pairs = [(i, i + by) for i in range(count) if 0 <= i + by < count]
    return lax.ppermute(value, axis, pairs)


def contract_rows(left, piece):
    return jnp.dot(left, piece, preferred_element_type=jnp.float32)


def contract_columns(whole, first, count, piece):
    block = lax.dynamic_slice(whole, (0, first), (piece.shape[0], count))
    return lax.dot_general(
        block, piece, (((0,), (0,)), ((), ())), preferred_element_type=jnp.float32
    )


def level_step(element, distance, first):
    a_own, c_own, j_own = element
    rows, width = a_own.shape
    a_part, c_part, j_prev = passed_along((a_own, c_own, j_own), "tm", distance)
    a_prev, c_prev = (
        lax.all_gather(a_part, "panel", axis=0, tiled=True),
        lax.all_gather(c_part, "panel", axis=0, tiled=True),
    )
    a_full, j_full = (
        lax.all_gather(a_own, "panel", axis=0, tiled=True),
        lax.all_gather(j_own, "panel", axis=0, tiled=True),
    )
    k_rows = jnp.dot(c_part, j_full, preferred_element_type=jnp.float32).astype(jnp.bfloat16)
    q_rows = contract_rows(k_rows, lax.all_gather(k_rows, "panel", axis=0, tiled=True)).astype(
        jnp.bfloat16
    )
    k_q = contract_rows(k_rows, lax.all_gather(q_rows, "panel", axis=0, tiled=True))
    row_ids = first + jnp.arange(rows, dtype=jnp.int32)
    identity = (row_ids[:, None] == jnp.arange(width, dtype=jnp.int32)[None, :]).astype(jnp.float32)
    x_rows = (identity - k_rows.astype(jnp.float32) + q_rows.astype(jnp.float32) - k_q).astype(
        jnp.bfloat16
    )
    u_rows = jnp.dot(x_rows, a_prev, preferred_element_type=jnp.float32).astype(jnp.bfloat16)
    a_sum = contract_rows(a_own, lax.all_gather(u_rows, "panel", axis=0, tiled=True))
    s_sum = contract_rows(j_own, lax.all_gather(u_rows, "panel", axis=0, tiled=True))
    a_new = a_sum.astype(jnp.bfloat16)
    s_rows = s_sum.astype(jnp.bfloat16)
    v_rows = jnp.dot(x_rows, c_prev, preferred_element_type=jnp.float32).astype(jnp.bfloat16)
    w_rows = contract_rows(a_own, lax.all_gather(v_rows, "panel", axis=0, tiled=True)).astype(
        jnp.bfloat16
    )
    c_sum = lax.dot_general(
        w_rows, a_full, (((1,), (1,)), ((), ())), preferred_element_type=jnp.float32
    )
    c_new = (c_sum + c_own.astype(jnp.float32)).astype(jnp.bfloat16)
    j_sum = contract_columns(
        a_prev, first, rows, lax.all_gather(s_rows, "panel", axis=0, tiled=True)
    )
    j_new = (j_sum + j_prev.astype(jnp.float32)).astype(jnp.bfloat16)
    valid = lax.axis_index("tm") >= distance
    return (
        jnp.where(valid, a_new, a_own),
        jnp.where(valid, c_new, c_own),
        jnp.where(valid, j_new, j_own),
    )


def shards(dynamics, coupling, cost_matrix, band_offset, band_width):
    rows = dynamics.shape[1]
    width = dynamics.shape[2]
    first = lax.axis_index("panel") * rows
    row_block = (first + jnp.arange(rows, dtype=jnp.int32)) // BLOCK
    block_ids = jnp.arange(width // BLOCK, dtype=jnp.int32)
    picked = row_block[:, None] == block_ids[None, :]
    offsets = jnp.sum(jnp.where(picked, band_offset[0][None, :], 0), axis=1)
    widths = jnp.sum(jnp.where(picked, band_width[0][None, :], 0), axis=1)
    col_block = jnp.arange(width, dtype=jnp.int32) // BLOCK
    lower = row_block + offsets
    inside = (col_block[None, :] >= lower[:, None]) & (
        col_block[None, :] < (lower + widths)[:, None]
    )
    c_start = jnp.where(inside, coupling[0], jnp.zeros_like(coupling[0]))
    element = (dynamics[0], c_start, cost_matrix[0])
    results = []
    for level in range(LEVELS):
        element = level_step(element, 2**level, first)
        results.append(jnp.stack(element, axis=0)[None])
    return (results[0], results[1])


def solution(mesh):
    in_specs = (
        P("tm", "panel", None),
        P("tm", "panel", None),
        P("tm", "panel", None),
        P("tm", None),
        P("tm", None),
    )
    out_specs = (P("tm", None, "panel", None), P("tm", None, "panel", None))
    return jax.shard_map(shards, mesh=mesh, in_specs=in_specs, out_specs=out_specs, check_vma=False)
```

profile of v0, /device:TPU:1, one launch (start us, length us, event | category | flops | bytes accessed | tf_op | source)
XLA Modules:
  0.0 1131.7 jit_solution(3765280901157855510)
XLA Ops:
  7.2 0.7 all-gather.53.cloned.1.call-update
  8.0 0.8 select_reduce_fusion
  8.8 1.1 and_select_fusion
  9.9 4.9 collective-permute-start
  14.8 3.6 collective-permute-done
  18.5 54.4 %all-gather.53.cloned.1.call-done = bf16[1,1536,1536]{2,1,0:T(8,128)(2,1)} async-done(((bf16[1,96,1536]{2,1,0:T(8,128)(2,1)}), bf16[1,1536,1536]{2,1,0:T(8,128)(2,1)}) %all-gather.53.cloned.1.call-update) | async-done | bytes 4718608 | tf_op jit(solution)/shard_map/all_gather | solution.py:37
  72.9 3.9 fusion.15
  76.8 0.0 all-gather.23.cloned.1.call-start
  76.9 58.7 %all-gather.21.cloned.1.call-done = bf16[1536,1536]{1,0:T(8,128)(2,1)} async-done(((bf16[96,1536]{1,0:T(8,128)(2,1)}), bf16[1536,1536]{1,0:T(8,128)(2,1)}) %all-gather.21.cloned.1.call-update) | async-done | bytes 4718608 | tf_op jit(solution)/shard_map/all_gather | solution.py:40
  135.5 4.0 convolution_convert_fusion.12
  139.6 0.0 all-gather.25.cloned.1.call-start
  139.7 3.9 collective-permute-start.1
  143.6 3.6 collective-permute-done.1
  147.2 0.7 copy-done.12
  148.0 0.0 all-gather.27.cloned.1.call-start
  148.0 50.3 %all-gather.23.cloned.1.call-done = bf16[1536,1536]{1,0:T(8,128)(2,1)} async-done(((bf16[96,1536]{1,0:T(8,128)(2,1)}), bf16[1536,1536]{1,0:T(8,128)(2,1)}) %all-gather.23.cloned.1.call-update) | async-done | bytes 4718608 | tf_op jit(solution)/shard_map/all_gather | solution.py:43
  198.3 3.3 fusion.7
  201.6 57.6 %all-gather.25.cloned.1.call-done = bf16[1536,1536]{1,0:T(8,128)(2,1)} async-done(((bf16[96,1536]{1,0:T(8,128)(2,1)}), bf16[1536,1536]{1,0:T(8,128)(2,1)}) %all-gather.25.cloned.1.call-update) | async-done | bytes 4718608 | tf_op jit(solution)/shard_map/all_gather | solution.py:32
  259.2 3.9 convolution_convert_fusion.11
  263.1 0.0 all-gather.29.cloned.1.call-start
  263.2 0.5 all-gather.29.cloned.1.call-update
  263.8 58.1 %all-gather.27.cloned.1.call-done = bf16[1536,1536]{1,0:T(8,128)(2,1)} async-done(((bf16[96,1536]{1,0:T(8,128)(2,1)}), bf16[1536,1536]{1,0:T(8,128)(2,1)}) %all-gather.27.cloned.1.call-update) | async-done | bytes 4718608 | tf_op jit(solution)/shard_map/all_gather | solution.py:50
  321.8 3.9 fusion.27
  325.8 0.0 all-gather.55.cloned.1.call-start
  325.9 0.7 all-gather.55.cloned.1.call-update
  326.6 56.1 %all-gather.29.cloned.1.call-done = bf16[1536,1536]{1,0:T(8,128)(2,1)} async-done(((bf16[96,1536]{1,0:T(8,128)(2,1)}), bf16[1536,1536]{1,0:T(8,128)(2,1)}) %all-gather.29.cloned.1.call-update) | async-done | bytes 4718608 | tf_op jit(solution)/shard_map/all_gather | solution.py:33
  382.7 3.9 convolution_convert_fusion.10
  386.7 3.9 collective-permute-start.2
  390.6 3.6 collective-permute-done.2
  394.3 50.0 %all-gather.33.cloned.1.call-done = bf16[1536,1536]{1,0:T(8,128)(2,1)} async-done(((bf16[96,1536]{1,0:T(8,128)(2,1)}), bf16[1536,1536]{1,0:T(8,128)(2,1)}) %all-gather.33.cloned.1.call-update) | async-done | bytes 4718608 | tf_op jit(solution)/shard_map/all_gather | solution.py:63
  444.3 4.3 fusion.21
  448.7 56.6 %all-gather.55.cloned.1.call-done = bf16[1,1536,1536]{2,1,0:T(8,128)(2,1)} async-done(((bf16[1,96,1536]{2,1,0:T(8,128)(2,1)}), bf16[1,1536,1536]{2,1,0:T(8,128)(2,1)}) %all-gather.55.cloned.1.call-update) | async-done | bytes 4718608 | tf_op jit(solution)/shard_map/all_gather | solution.py:36
  505.3 61.6 %all-gather.31.cloned.1.call-done = bf16[1536,1536]{1,0:T(8,128)(2,1)} async-done(((bf16[96,1536]{1,0:T(8,128)(2,1)}), bf16[1536,1536]{1,0:T(8,128)(2,1)}) %all-gather.31.cloned.1.call-update) | async-done | bytes 4718608 | tf_op jit(solution)/shard_map/all_gather | solution.py:55
  566.9 6.1 fusion.28
  573.0 3.2 collective-permute-start.3
  576.2 5.5 collective-permute-done.3
  581.7 46.6 %all-gather.35.cloned.1.call-done = bf16[1536,1536]{1,0:T(8,128)(2,1)} async-done(((bf16[96,1536]{1,0:T(8,128)(2,1)}), bf16[1536,1536]{1,0:T(8,128)(2,1)}) %all-gather.35.cloned.1.call-update) | async-done | bytes 4718608 | tf_op jit(solution)/shard_map/all_gather | solution.py:37
  628.3 3.9 convolution_convert_fusion.9
  632.3 0.0 all-gather.39.cloned.1.call-start
  632.3 58.6 %all-gather.37.cloned.1.call-done = bf16[1536,1536]{1,0:T(8,128)(2,1)} async-done(((bf16[96,1536]{1,0:T(8,128)(2,1)}), bf16[1536,1536]{1,0:T(8,128)(2,1)}) %all-gather.37.cloned.1.call-update) | async-done | bytes 4718608 | tf_op jit(solution)/shard_map/all_gather | solution.py:40
  691.0 4.0 convolution_convert_fusion.8
  695.1 3.3 fusion.26
  698.4 3.2 collective-permute-start.4
  701.6 5.5 collective-permute-done.4
  707.1 0.7 copy-done.11
  707.9 0.5 all-gather.45.cloned.1.call-update
  708.4 45.3 %all-gather.39.cloned.1.call-done = bf16[1536,1536]{1,0:T(8,128)(2,1)} async-done(((bf16[96,1536]{1,0:T(8,128)(2,1)}), bf16[1536,1536]{1,0:T(8,128)(2,1)}) %all-gather.39.cloned.1.call-update) | async-done | bytes 4718608 | tf_op jit(solution)/shard_map/all_gather | solution.py:43
  753.8 3.2 fusion.9
  757.0 57.8 %all-gather.41.cloned.1.call-done = bf16[1536,1536]{1,0:T(8,128)(2,1)} async-done(((bf16[96,1536]{1,0:T(8,128)(2,1)}), bf16[1536,1536]{1,0:T(8,128)(2,1)}) %all-gather.41.cloned.1.call-update) | async-done | bytes 4718608 | tf_op jit(solution)/shard_map/all_gather | solution.py:32
  814.8 3.9 convolution_convert_fusion.7
  818.8 0.5 all-gather.49.cloned.1.call-update
  819.4 56.3 %all-gather.45.cloned.1.call-done = bf16[1536,1536]{1,0:T(8,128)(2,1)} async-done(((bf16[96,1536]{1,0:T(8,128)(2,1)}), bf16[1536,1536]{1,0:T(8,128)(2,1)}) %all-gather.45.cloned.1.call-update) | async-done | bytes 4718608 | tf_op jit(solution)/shard_map/all_gather | solution.py:33
  875.6 4.0 convolution_convert_fusion.5
  879.7 57.4 %all-gather.43.cloned.1.call-done = bf16[1536,1536]{1,0:T(8,128)(2,1)} async-done(((bf16[96,1536]{1,0:T(8,128)(2,1)}), bf16[1536,1536]{1,0:T(8,128)(2,1)}) %all-gather.43.cloned.1.call-update) | async-done | bytes 4718608 | tf_op jit(solution)/shard_map/all_gather | solution.py:50
  937.1 3.9 convolution_convert_fusion.3
  941.0 3.4 collective-permute-start.5
  944.4 1.0 maximum_bitcast_fusion
  945.4 52.5 %all-gather.49.cloned.1.call-done = bf16[1536,1536]{1,0:T(8,128)(2,1)} async-done(((bf16[96,1536]{1,0:T(8,128)(2,1)}), bf16[1536,1536]{1,0:T(8,128)(2,1)}) %all-gather.49.cloned.1.call-update) | async-done | bytes 4718608 | tf_op jit(solution)/shard_map/all_gather | solution.py:36
  997.9 60.9 %all-gather.47.cloned.1.call-done = bf16[1536,1536]{1,0:T(8,128)(2,1)} async-done(((bf16[96,1536]{1,0:T(8,128)(2,1)}), bf16[1536,1536]{1,0:T(8,128)(2,1)}) %all-gather.47.cloned.1.call-update) | async-done | bytes 4718608 | tf_op jit(solution)/shard_map/all_gather | solution.py:55
  1058.8 6.1 fusion.22
  1064.9 3.2 fusion.24
  1068.1 52.1 %all-gather.51.cloned.1.call-done = bf16[1536,1536]{1,0:T(8,128)(2,1)} async-done(((bf16[96,1536]{1,0:T(8,128)(2,1)}), bf16[1536,1536]{1,0:T(8,128)(2,1)}) %all-gather.51.cloned.1.call-update) | async-done | bytes 4718608 | tf_op jit(solution)/shard_map/all_gather | solution.py:63
  1120.2 3.6 fusion.23
  1123.8 1.0 maximum_bitcast_fusion.1
  (54 shorter events, 0.8 us)
Async XLA Ops:
  7.2 65.7 %all-gather.53.cloned.1.call-start = ((), (), s32[]{:S(2)}) async-start(), calls=%async_computation.16 | async-start | bytes 5013504 | tf_op jit(solution)/shard_map/all_gather | solution.py:37
  7.9 127.6 %all-gather.21.cloned.1.call-start = ((), (), s32[]{:S(2)}) async-start(), calls=%async_computation | async-start | bytes 5013504 | tf_op jit(solution)/shard_map/all_gather | solution.py:40
  9.9 8.6 collective-permute-start
  18.5 121.1 %copy-start.9 = (bf16[96,1536]{1,0:T(8,128)(2,1)}, bf16[96,1536]{1,0:T(8,128)(2,1)S(1)}, u32[]{:S(2)}) copy-start(bf16[96,1536]{1,0:T(8,128)(2,1)S(1)} %collective-permute-done) | copy-start | bytes 884740
  18.5 121.2 %copy-start.7 = (bf16[1,96,1536]{2,1,0:T(8,128)(2,1)S(1)}, bf16[1,96,1536]{2,1,0:T(8,128)(2,1)}, u32[]{:S(2)}) copy-start(bf16[1,96,1536]{2,1,0:T(8,128)(2,1)} %param.5) | copy-start | bytes 884740
  76.8 121.5 %copy-start.4 = (bf16[96,1536]{1,0:T(8,128)(2,1)S(1)}, bf16[96,1536]{1,0:T(8,128)(2,1)}, u32[]{:S(2)}) copy-start(bf16[96,1536]{1,0:T(8,128)(2,1)} %fusion.15) | copy-start | bytes 884740
  76.8 121.5 %all-gather.23.cloned.1.call-start = ((), (), s32[]{:S(2)}) async-start(), calls=%async_computation.1 | async-start | bytes 5013504 | tf_op jit(solution)/shard_map/all_gather | solution.py:43
  139.6 119.6 %all-gather.25.cloned.1.call-start = ((), (), s32[]{:S(2)}) async-start(), calls=%async_computation.2 | async-start | bytes 5013504 | tf_op jit(solution)/shard_map/all_gather | solution.py:32
  139.7 7.6 collective-permute-start.1
  147.2 0.7 copy-start.12
  148.0 173.9 %all-gather.27.cloned.1.call-start = ((), (), s32[]{:S(2)}) async-start(), calls=%async_computation.3 | async-start | bytes 5013504 | tf_op jit(solution)/shard_map/all_gather | solution.py:50
  148.0 173.8 %copy-start.5 = (bf16[1,96,1536]{2,1,0:T(8,128)(2,1)S(1)}, bf16[1,96,1536]{2,1,0:T(8,128)(2,1)}, u32[]{:S(2)}) copy-start(bf16[1,96,1536]{2,1,0:T(8,128)(2,1)} %param.7) | copy-start | bytes 884740
  263.1 119.6 %all-gather.29.cloned.1.call-start = ((), (), s32[]{:S(2)}) async-start(), calls=%async_computation.4 | async-start | bytes 5013504 | tf_op jit(solution)/shard_map/all_gather | solution.py:33
  263.7 180.6 %all-gather.33.cloned.1.call-start = ((), (), s32[]{:S(2)}) async-start(), calls=%async_computation.6 | async-start | bytes 5013504 | tf_op jit(solution)/shard_map/all_gather | solution.py:63
  325.8 179.5 %all-gather.55.cloned.1.call-start = ((), (), s32[]{:S(2)}) async-start(), calls=%async_computation.17 | async-start | bytes 5013504 | tf_op jit(solution)/shard_map/all_gather | solution.py:36
  326.6 240.3 %copy-start.8 = (bf16[1,96,1536]{2,1,0:T(8,128)(2,1)S(1)}, bf16[1,96,1536]{2,1,0:T(8,128)(2,1)}, u32[]{:S(2)}) copy-start(bf16[1,96,1536]{2,1,0:T(8,128)(2,1)} %param.5) | copy-start | bytes 884740
  326.6 240.3 %all-gather.31.cloned.1.call-start = ((), (), s32[]{:S(2)}) async-start(), calls=%async_computation.5 | async-start | bytes 5013504 | tf_op jit(solution)/shard_map/all_gather | solution.py:55
  386.7 241.7 %all-gather.35.cloned.1.call-start = ((), (), s32[]{:S(2)}) async-start(), calls=%async_computation.7 | async-start | bytes 5013504 | tf_op jit(solution)/shard_map/all_gather | solution.py:37
  386.7 7.6 collective-permute-start.2
  448.6 242.4 %all-gather.37.cloned.1.call-start = ((), (), s32[]{:S(2)}) async-start(), calls=%async_computation.8 | async-start | bytes 5013504 | tf_op jit(solution)/shard_map/all_gather | solution.py:40
  573.0 8.7 collective-permute-start.3
  581.7 113.3 %copy-start.10 = (bf16[96,1536]{1,0:T(8,128)(2,1)}, bf16[96,1536]{1,0:T(8,128)(2,1)S(1)}, u32[]{:S(2)}) copy-start(bf16[96,1536]{1,0:T(8,128)(2,1)S(1)} %collective-permute-done.3) | copy-start | bytes 884740
  632.3 121.5 %copy-start.3 = (bf16[96,1536]{1,0:T(8,128)(2,1)S(1)}, bf16[96,1536]{1,0:T(8,128)(2,1)}, u32[]{:S(2)}) copy-start(bf16[96,1536]{1,0:T(8,128)(2,1)} %convolution_convert_fusion.9) | copy-start | bytes 884740
  632.3 121.5 %all-gather.39.cloned.1.call-start = ((), (), s32[]{:S(2)}) async-start(), calls=%async_computation.9 | async-start | bytes 5013504 | tf_op jit(solution)/shard_map/all_gather | solution.py:43
  695.0 58.7 %copy-start.6 = (bf16[96,1536]{1,0:T(8,128)(2,1)S(1)}, bf16[96,1536]{1,0:T(8,128)(2,1)}, u32[]{:S(2)}) copy-start(bf16[96,1536]{1,0:T(8,128)(2,1)} %convolution_convert_fusion.8) | copy-start | bytes 884740
  695.1 119.7 %all-gather.41.cloned.1.call-start = ((), (), s32[]{:S(2)}) async-start(), calls=%async_computation.10 | async-start | bytes 5013504 | tf_op jit(solution)/shard_map/all_gather | solution.py:32
  698.4 120.3 %copy-start.1 = (bf16[96,1536]{1,0:T(8,128)(2,1)}, bf16[96,1536]{1,0:T(8,128)(2,1)S(1)}, u32[]{:S(2)}) copy-start(bf16[96,1536]{1,0:T(8,128)(2,1)S(1)} %fusion.26) | copy-start | bytes 884740
  698.4 8.7 collective-permute-start.4
  707.1 0.7 copy-start.11
  707.8 167.8 %all-gather.45.cloned.1.call-start = ((), (), s32[]{:S(2)}) async-start(), calls=%async_computation.12 | async-start | bytes 5013504 | tf_op jit(solution)/shard_map/all_gather | solution.py:33
  708.4 228.7 %all-gather.43.cloned.1.call-start = ((), (), s32[]{:S(2)}) async-start(), calls=%async_computation.11 | async-start | bytes 5013504 | tf_op jit(solution)/shard_map/all_gather | solution.py:50
  757.0 180.1 %copy-start = (bf16[96,1536]{1,0:T(8,128)(2,1)S(1)}, bf16[96,1536]{1,0:T(8,128)(2,1)}, u32[]{:S(2)}) copy-start(bf16[96,1536]{1,0:T(8,128)(2,1)} %fusion.21) | copy-start | bytes 884740
  818.7 179.2 %all-gather.49.cloned.1.call-start = ((), (), s32[]{:S(2)}) async-start(), calls=%async_computation.14 | async-start | bytes 5013504 | tf_op jit(solution)/shard_map/all_gather | solution.py:36
  819.3 125.1 %copy-start.2 = (bf16[96,1536]{1,0:T(8,128)(2,1)S(1)}, bf16[96,1536]{1,0:T(8,128)(2,1)}, u32[]{:S(2)}) copy-start(bf16[96,1536]{1,0:T(8,128)(2,1)} %copy-done.1) | copy-start | bytes 884740
  819.3 239.5 %all-gather.47.cloned.1.call-start = ((), (), s32[]{:S(2)}) async-start(), calls=%async_computation.13 | async-start | bytes 5013504 | tf_op jit(solution)/shard_map/all_gather | solution.py:55
  879.6 240.6 %all-gather.51.cloned.1.call-start = ((), (), s32[]{:S(2)}) async-start(), calls=%async_computation.15 | async-start | bytes 5013504 | tf_op jit(solution)/shard_map/all_gather | solution.py:63
  941.0 127.1 %collective-permute-start.5 = (bf16[96,1536]{1,0:T(8,128)(2,1)S(1)}, bf16[96,1536]{1,0:T(8,128)(2,1)S(1)}, u32[]{:S(2)}, u32[]{:S(2)}) collective-permute-start(bf16[96,1536]{1,0:T(8,128)(2,1)S(1)} %copy-done), channel_id=1, source_target_pairs={{0,32},{16,48},{32,64},{48,80},{64,96},{80,112},{96,128},{112,144}... | collective-permute-start | bytes 884744 | tf_op jit(solution)/shard_map/ppermute | solution.py:13
Sparse Core Ops, SparseCore 0:
  10.4 62.4 all-gather.52
  76.9 58.5 all-gather.20
  139.7 58.5 all-gather.22
  200.6 58.5 all-gather.24
  263.3 58.5 all-gather.26
  324.1 58.5 all-gather.28
  385.7 58.5 all-gather.32
  446.7 58.5 all-gather.54
  508.3 58.5 all-gather.30
  569.7 58.5 all-gather.34
  632.4 58.5 all-gather.36
  695.2 58.5 all-gather.38
  756.2 58.5 all-gather.40
  817.1 58.5 all-gather.44
  878.5 58.5 all-gather.42
  939.4 58.5 all-gather.48
  1000.2 58.5 all-gather.46
  1061.7 58.5 all-gather.50
where the time goes:
time: 1130 us
  waiting for transfers between devices  1020 us (90%)
  matrix products  72.6 us (6%)
  starting transfers between devices  23.2 us (2%)
  between operations  14.5 us (1%)
    all_gather x2, waiting for transfers between devices, level_step(): lax.all_gather(v_rows, 'panel', axis=0, tiled=True)  122 us
    all_gather x2, waiting for transfers between devices, level_step(): lax.all_gather(k_rows, 'panel', axis=0, tiled=True)  117 us
    all_gather x2, waiting for transfers between devices, level_step(): lax.all_gather(u_rows, 'panel', axis=0, tiled=True)  115 us
    all_gather x2, waiting for transfers between devices, level_step(): lax.all_gather(a_part, 'panel', axis=0, tiled=True)  115 us
    all_gather x2, waiting for transfers between devices, level_step(): lax.all_gather(c_part, 'panel', axis=0, tiled=True)  112 us
    all_gather x2, waiting for transfers between devices, level_step(): lax.all_gather(a_own, 'panel', axis=0, tiled=True)  109 us
    all_gather x2, waiting for transfers between devices, level_step(): lax.all_gather(s_rows, 'panel', axis=0, tiled=True)  102 us
    all_gather x2, waiting for transfers between devices, level_step(): lax.all_gather(j_own, 'panel', axis=0, tiled=True)  101 us
  transfers between devices with their start and end apart: 24, of which 23 were waited for; matrix products, arithmetic and copies ran while one was open for 5% of the time, Pallas kernels for 0%

commit v1 on v0

--- a/solution.py
+++ b/solution.py
@@ -5,6 +5,19 @@
 
 BLOCK = 128
 LEVELS = 2
+
+
+def ring_gather(x, axis, dim):
+    ways = lax.axis_size(axis)
+    up = [(d, (d + 1) % ways) for d in range(ways)]
+    down = [(d, (d - 1) % ways) for d in range(ways)]
+    earlier, later = ([x], [x])
+    for _ in range(ways // 2):
+        earlier.append(lax.ppermute(earlier[-1], axis, up))
+    for _ in range((ways - 1) // 2):
+        later.append(lax.ppermute(later[-1], axis, down))
+    line = jnp.concatenate([*earlier[::-1], *later[1:]], axis=dim)
+    return jnp.roll(line, (lax.axis_index(axis) - ways // 2) * x.shape[dim], axis=dim)
 
 
 def passed_along(value, axis, by):
@@ -37,9 +50,7 @@
         lax.all_gather(j_own, "panel", axis=0, tiled=True),
     )
     k_rows = jnp.dot(c_part, j_full, preferred_element_type=jnp.float32).astype(jnp.bfloat16)
-    q_rows = contract_rows(k_rows, lax.all_gather(k_rows, "panel", axis=0, tiled=True)).astype(
-        jnp.bfloat16
-    )
+    q_rows = contract_rows(k_rows, ring_gather(k_rows, "panel", 0)).astype(jnp.bfloat16)
     k_q = contract_rows(k_rows, lax.all_gather(q_rows, "panel", axis=0, tiled=True))
     row_ids = first + jnp.arange(rows, dtype=jnp.int32)
     identity = (row_ids[:, None] == jnp.arange(width, dtype=jnp.int32)[None, :]).astype(jnp.float32)

time: 1130 us -> 1200 us (1.062)
  starting transfers between devices: 23.2 us -> 102 us
  waiting for transfers between devices: 1020 us -> 990 us
    all_gather x2 -> x0, waiting for transfers between devices: 117 us -> none  [level_step(): lax.all_gather(k_rows, 'panel', axis=0, tiled=True)]
    ppermute x0 -> x30, waiting for transfers between devices: none -> 83.6 us  [the longest x16 83.6 us: ring_gather(): earlier.append(lax.ppermute(earlier[-1], axis, up))]
    ppermute x0 -> x30, starting transfers between devices: none -> 70.9 us  [the longest x14 68.1 us: ring_gather(): later.append(lax.ppermute(later[-1], axis, down))]
  transfers between devices with their start and end apart: 24 -> 52, of which waited for: 23 -> 37; matrix products, arithmetic and copies ran while one was open for 5% -> 5% of each run, Pallas kernels for 0% -> 0%
where the time goes in v1:
time: 1200 us; the launch traced here: 1190 us
  waiting for transfers between devices  990 us (82%)
  starting transfers between devices  102 us (8%)
  matrix products  72.6 us (6%)
  between operations  14.7 us (1%)
    all_gather x2, waiting for transfers between devices, level_step(): lax.all_gather(v_rows, 'panel', axis=0, tiled=True)  122 us
    all_gather x2, waiting for transfers between devices, level_step(): lax.all_gather(a_part, 'panel', axis=0, tiled=True)  116 us
    all_gather x2, waiting for transfers between devices, level_step(): lax.all_gather(u_rows, 'panel', axis=0, tiled=True)  116 us
    all_gather x2, waiting for transfers between devices, level_step(): lax.all_gather(c_part, 'panel', axis=0, tiled=True)  112 us
    all_gather x2, waiting for transfers between devices, level_step(): lax.all_gather(a_own, 'panel', axis=0, tiled=True)  109 us
    all_gather x2, waiting for transfers between devices, level_step(): lax.all_gather(q_rows, 'panel', axis=0, tiled=True)  104 us
    all_gather x2, waiting for transfers between devices, level_step(): lax.all_gather(s_rows, 'panel', axis=0, tiled=True)  102 us
    all_gather x2, waiting for transfers between devices, level_step(): lax.all_gather(j_own, 'panel', axis=0, tiled=True)  101 us
  transfers between devices with their start and end apart: 52, of which 37 were waited for; matrix products, arithmetic and copies ran while one was open for 5% of the time, Pallas kernels for 0%

profile of v1, /device:TPU:1, one launch (start us, length us, event | category | flops | bytes accessed | tf_op | source)
XLA Modules:
  0.0 1190.2 jit_solution(13725953595227496020)
XLA Ops:
  9.9 4.9 collective-permute-start
  14.8 3.6 collective-permute-done
  18.5 54.4 %all-gather.47.cloned.1.call-done = bf16[1,1536,1536]{2,1,0:T(8,128)(2,1)} async-done(((bf16[1,96,1536]{2,1,0:T(8,128)(2,1)}), bf16[1,1536,1536]{2,1,0:T(8,128)(2,1)}) %all-gather.47.cloned.1.call-update) | async-done | bytes 4718608 | tf_op jit(solution)/shard_map/all_gather | solution.py:50
  77.4 9.9 collective-permute-done.1
  87.2 4.8 collective-permute-start.9
  92.0 5.4 collective-permute-done.2
  97.4 4.8 collective-permute-start.10
  102.2 4.5 collective-permute-done.3
  106.7 4.8 collective-permute-start.11
  111.5 4.1 collective-permute-done.4
  115.6 4.8 collective-permute-start.12
  120.4 4.1 collective-permute-done.5
  124.5 4.8 collective-permute-start.13
  129.3 4.1 collective-permute-done.6
  133.4 4.8 collective-permute-start.14
  138.2 4.6 collective-permute-done.7
  142.9 5.5 collective-permute-start.15
  148.4 5.0 collective-permute-done.8
  158.6 4.8 fusion.22
  163.5 12.2 %collective-permute-start.16 = (bf16[96,1536]{1,0:T(8,128)(2,1)S(1)}, bf16[96,1536]{1,0:T(8,128)(2,1)S(1)}, u32[]{:S(2)}, u32[]{:S(2)}) collective-permute-start(bf16[96,1536]{1,0:T(8,128)(2,1)S(1)} %bitcast.79), channel_id=1, source_target_pairs={{0,16},{16,32},{32,48},{48,64},{64,80},{80,96},{96,112},{112,128},... | collective-permute-start | bytes 884744 | tf_op jit(solution)/shard_map/ppermute | solution.py:26
  175.7 3.6 collective-permute-done.16
  180.2 47.0 %all-gather.19.cloned.1.call-done = bf16[1536,1536]{1,0:T(8,128)(2,1)} async-done(((bf16[96,1536]{1,0:T(8,128)(2,1)}), bf16[1536,1536]{1,0:T(8,128)(2,1)}) %all-gather.19.cloned.1.call-update) | async-done | bytes 4718608 | tf_op jit(solution)/shard_map/all_gather | solution.py:54
  230.4 58.3 %all-gather.21.cloned.1.call-done = bf16[1536,1536]{1,0:T(8,128)(2,1)} async-done(((bf16[96,1536]{1,0:T(8,128)(2,1)}), bf16[1536,1536]{1,0:T(8,128)(2,1)}) %all-gather.21.cloned.1.call-update) | async-done | bytes 4718608 | tf_op jit(solution)/shard_map/all_gather | solution.py:45
  288.7 3.9 convolution_convert_fusion.10
  293.3 58.1 %all-gather.23.cloned.1.call-done = bf16[1536,1536]{1,0:T(8,128)(2,1)} async-done(((bf16[96,1536]{1,0:T(8,128)(2,1)}), bf16[1536,1536]{1,0:T(8,128)(2,1)}) %all-gather.23.cloned.1.call-update) | async-done | bytes 4718608 | tf_op jit(solution)/shard_map/all_gather | solution.py:61
  351.4 3.9 fusion.37
  356.2 56.1 %all-gather.25.cloned.1.call-done = bf16[1536,1536]{1,0:T(8,128)(2,1)} async-done(((bf16[96,1536]{1,0:T(8,128)(2,1)}), bf16[1536,1536]{1,0:T(8,128)(2,1)}) %all-gather.25.cloned.1.call-update) | async-done | bytes 4718608 | tf_op jit(solution)/shard_map/all_gather | solution.py:46
  412.2 3.9 convolution_convert_fusion.9
  416.2 3.9 collective-permute-start.17
  420.2 3.6 collective-permute-done.17
  423.8 49.9 %all-gather.29.cloned.1.call-done = bf16[1536,1536]{1,0:T(8,128)(2,1)} async-done(((bf16[96,1536]{1,0:T(8,128)(2,1)}), bf16[1536,1536]{1,0:T(8,128)(2,1)}) %all-gather.29.cloned.1.call-update) | async-done | bytes 4718608 | tf_op jit(solution)/shard_map/all_gather | solution.py:74
  473.7 4.3 fusion.31
  478.1 56.6 %all-gather.49.cloned.1.call-done = bf16[1,1536,1536]{2,1,0:T(8,128)(2,1)} async-done(((bf16[1,96,1536]{2,1,0:T(8,128)(2,1)}), bf16[1,1536,1536]{2,1,0:T(8,128)(2,1)}) %all-gather.49.cloned.1.call-update) | async-done | bytes 4718608 | tf_op jit(solution)/shard_map/all_gather | solution.py:49
  534.7 61.6 %all-gather.27.cloned.1.call-done = bf16[1536,1536]{1,0:T(8,128)(2,1)} async-done(((bf16[96,1536]{1,0:T(8,128)(2,1)}), bf16[1536,1536]{1,0:T(8,128)(2,1)}) %all-gather.27.cloned.1.call-update) | async-done | bytes 4718608 | tf_op jit(solution)/shard_map/all_gather | solution.py:66
  596.3 6.1 fusion.38
  605.6 5.5 collective-permute-done.18
  611.0 46.8 %all-gather.31.cloned.1.call-done = bf16[1536,1536]{1,0:T(8,128)(2,1)} async-done(((bf16[96,1536]{1,0:T(8,128)(2,1)}), bf16[1536,1536]{1,0:T(8,128)(2,1)}) %all-gather.31.cloned.1.call-update) | async-done | bytes 4718608 | tf_op jit(solution)/shard_map/all_gather | solution.py:50
  662.3 9.9 collective-permute-done.19
  672.4 4.8 collective-permute-start.27
  677.1 5.4 collective-permute-done.20
  682.5 4.8 collective-permute-start.28
  687.3 4.5 collective-permute-done.21
  691.9 4.8 collective-permute-start.29
  696.7 4.1 collective-permute-done.22
  700.8 4.8 collective-permute-start.30
  705.6 4.1 collective-permute-done.23
  709.7 4.8 collective-permute-start.31
  714.4 4.1 collective-permute-done.24
  718.6 4.8 collective-permute-start.32
  723.3 4.5 collective-permute-done.25
  727.9 5.3 collective-permute-start.33
  733.1 5.2 collective-permute-done.26
  738.8 4.8 fusion.19
  755.2 57.1 %all-gather.33.cloned.1.call-done = bf16[1536,1536]{1,0:T(8,128)(2,1)} async-done(((bf16[96,1536]{1,0:T(8,128)(2,1)}), bf16[1536,1536]{1,0:T(8,128)(2,1)}) %all-gather.33.cloned.1.call-update) | async-done | bytes 4718608 | tf_op jit(solution)/shard_map/all_gather | solution.py:54
  815.5 57.8 %all-gather.35.cloned.1.call-done = bf16[1536,1536]{1,0:T(8,128)(2,1)} async-done(((bf16[96,1536]{1,0:T(8,128)(2,1)}), bf16[1536,1536]{1,0:T(8,128)(2,1)}) %all-gather.35.cloned.1.call-update) | async-done | bytes 4718608 | tf_op jit(solution)/shard_map/all_gather | solution.py:45
  873.3 3.9 convolution_convert_fusion.7
  877.9 56.3 %all-gather.39.cloned.1.call-done = bf16[1536,1536]{1,0:T(8,128)(2,1)} async-done(((bf16[96,1536]{1,0:T(8,128)(2,1)}), bf16[1536,1536]{1,0:T(8,128)(2,1)}) %all-gather.39.cloned.1.call-update) | async-done | bytes 4718608 | tf_op jit(solution)/shard_map/all_gather | solution.py:46
  934.1 3.9 convolution_convert_fusion.5
  938.1 57.6 %all-gather.37.cloned.1.call-done = bf16[1536,1536]{1,0:T(8,128)(2,1)} async-done(((bf16[96,1536]{1,0:T(8,128)(2,1)}), bf16[1536,1536]{1,0:T(8,128)(2,1)}) %all-gather.37.cloned.1.call-update) | async-done | bytes 4718608 | tf_op jit(solution)/shard_map/all_gather | solution.py:61
  995.7 3.9 convolution_convert_fusion.3
  1003.9 52.7 %all-gather.43.cloned.1.call-done = bf16[1536,1536]{1,0:T(8,128)(2,1)} async-done(((bf16[96,1536]{1,0:T(8,128)(2,1)}), bf16[1536,1536]{1,0:T(8,128)(2,1)}) %all-gather.43.cloned.1.call-update) | async-done | bytes 4718608 | tf_op jit(solution)/shard_map/all_gather | solution.py:49
  1056.6 60.9 %all-gather.41.cloned.1.call-done = bf16[1536,1536]{1,0:T(8,128)(2,1)} async-done(((bf16[96,1536]{1,0:T(8,128)(2,1)}), bf16[1536,1536]{1,0:T(8,128)(2,1)}) %all-gather.41.cloned.1.call-update) | async-done | bytes 4718608 | tf_op jit(solution)/shard_map/all_gather | solution.py:66
  1117.4 6.1 fusion.32
  1126.7 52.1 %all-gather.45.cloned.1.call-done = bf16[1536,1536]{1,0:T(8,128)(2,1)} async-done(((bf16[96,1536]{1,0:T(8,128)(2,1)}), bf16[1536,1536]{1,0:T(8,128)(2,1)}) %all-gather.45.cloned.1.call-update) | async-done | bytes 4718608 | tf_op jit(solution)/shard_map/all_gather | solution.py:74
  (140 shorter events, 53.7 us)
Async XLA Ops:
  7.2 65.7 %all-gather.47.cloned.1.call-start = ((), (), s32[]{:S(2)}) async-start(), calls=%async_computation.14 | async-start | bytes 5013504 | tf_op jit(solution)/shard_map/all_gather | solution.py:50
  7.9 219.2 %all-gather.19.cloned.1.call-start = ((), (), s32[]{:S(2)}) async-start(), calls=%async_computation | async-start | bytes 5013504 | tf_op jit(solution)/shard_map/all_gather | solution.py:54
  9.9 8.6 collective-permute-start
  18.5 138.9 %copy-start.7 = (bf16[96,1536]{1,0:T(8,128)(2,1)}, bf16[96,1536]{1,0:T(8,128)(2,1)S(1)}, u32[]{:S(2)}) copy-start(bf16[96,1536]{1,0:T(8,128)(2,1)S(1)} %collective-permute-done) | copy-start | bytes 884740
  76.1 11.1 collective-permute-start.1
  87.2 10.2 collective-permute-start.2
  87.2 10.2 collective-permute-start.9
  97.4 9.3 collective-permute-start.3
  97.4 9.3 collective-permute-start.10
  106.7 8.9 collective-permute-start.4
  106.7 8.9 collective-permute-start.11
  115.6 8.9 collective-permute-start.5
  115.6 8.9 collective-permute-start.12
  124.5 8.9 copy-start.9
  124.5 8.9 collective-permute-start.6
  124.5 8.9 collective-permute-start.13
  133.4 4.8 copy-start.10
  133.4 9.4 collective-permute-start.7
  133.4 9.4 collective-permute-start.14
  142.8 10.5 collective-permute-start.8
  142.9 15.7 %collective-permute-start.15 = (bf16[96,1536]{1,0:T(8,128)(2,1)}, bf16[96,1536]{1,0:T(8,128)(2,1)S(1)}, u32[]{:S(2)}, u32[]{:S(2)}) collective-permute-start(bf16[96,1536]{1,0:T(8,128)(2,1)} %collective-permute-done.14), channel_id=1, source_target_pairs={{0,15},{1,0},{2,1},{3,2},{4,3},{5,4},{6,5},{7,6},{8,7},{9,8},{10,9... | collective-permute-start | bytes 884744 | tf_op jit(solution)/shard_map/ppermute | solution.py:18
  158.6 4.9 copy-start.4
  163.4 125.3 %all-gather.21.cloned.1.call-start = ((), (), s32[]{:S(2)}) async-start(), calls=%async_computation.1 | async-start | bytes 5013504 | tf_op jit(solution)/shard_map/all_gather | solution.py:45
  163.5 15.9 %collective-permute-start.16 = (bf16[96,1536]{1,0:T(8,128)(2,1)S(1)}, bf16[96,1536]{1,0:T(8,128)(2,1)S(1)}, u32[]{:S(2)}, u32[]{:S(2)}) collective-permute-start(bf16[96,1536]{1,0:T(8,128)(2,1)S(1)} %bitcast.79), channel_id=1, source_target_pairs={{0,16},{16,32},{32,48},{48,64},{64,80},{80,96},{96,112},{112,128},... | collective-permute-start | bytes 884744 | tf_op jit(solution)/shard_map/ppermute | solution.py:26
  179.3 0.7 copy-start.12
  180.1 171.3 %all-gather.23.cloned.1.call-start = ((), (), s32[]{:S(2)}) async-start(), calls=%async_computation.2 | async-start | bytes 5013504 | tf_op jit(solution)/shard_map/all_gather | solution.py:61
  180.1 171.2 %copy-start.3 = (bf16[1,96,1536]{2,1,0:T(8,128)(2,1)S(1)}, bf16[1,96,1536]{2,1,0:T(8,128)(2,1)}, u32[]{:S(2)}) copy-start(bf16[1,96,1536]{2,1,0:T(8,128)(2,1)} %param.9) | copy-start | bytes 884740
  292.7 119.6 %all-gather.25.cloned.1.call-start = ((), (), s32[]{:S(2)}) async-start(), calls=%async_computation.3 | async-start | bytes 5013504 | tf_op jit(solution)/shard_map/all_gather | solution.py:46
  293.3 180.4 %all-gather.29.cloned.1.call-start = ((), (), s32[]{:S(2)}) async-start(), calls=%async_computation.5 | async-start | bytes 5013504 | tf_op jit(solution)/shard_map/all_gather | solution.py:74
  355.3 179.3 %all-gather.49.cloned.1.call-start = ((), (), s32[]{:S(2)}) async-start(), calls=%async_computation.15 | async-start | bytes 5013504 | tf_op jit(solution)/shard_map/all_gather | solution.py:49
  356.1 240.2 %copy-start.5 = (bf16[1,96,1536]{2,1,0:T(8,128)(2,1)S(1)}, bf16[1,96,1536]{2,1,0:T(8,128)(2,1)}, u32[]{:S(2)}) copy-start(bf16[1,96,1536]{2,1,0:T(8,128)(2,1)} %param.7) | copy-start | bytes 884740
  356.1 240.2 %all-gather.27.cloned.1.call-start = ((), (), s32[]{:S(2)}) async-start(), calls=%async_computation.4 | async-start | bytes 5013504 | tf_op jit(solution)/shard_map/all_gather | solution.py:66
  416.2 241.7 %all-gather.31.cloned.1.call-start = ((), (), s32[]{:S(2)}) async-start(), calls=%async_computation.6 | async-start | bytes 5013504 | tf_op jit(solution)/shard_map/all_gather | solution.py:50
  416.2 7.6 collective-permute-start.17
  478.0 334.2 %all-gather.33.cloned.1.call-start = ((), (), s32[]{:S(2)}) async-start(), calls=%async_computation.7 | async-start | bytes 5013504 | tf_op jit(solution)/shard_map/all_gather | solution.py:54
  602.4 8.7 collective-permute-start.18
  611.0 127.5 %copy-start.8 = (bf16[96,1536]{1,0:T(8,128)(2,1)}, bf16[96,1536]{1,0:T(8,128)(2,1)S(1)}, u32[]{:S(2)}) copy-start(bf16[96,1536]{1,0:T(8,128)(2,1)S(1)} %collective-permute-done.18) | copy-start | bytes 884740
  661.1 11.1 collective-permute-start.19
  672.2 10.3 collective-permute-start.20
  672.4 10.2 collective-permute-start.27
  682.5 9.3 collective-permute-start.21
  682.5 9.3 collective-permute-start.28
  691.9 8.9 collective-permute-start.22
  691.9 8.9 collective-permute-start.29
  700.8 8.9 collective-permute-start.23
  700.8 8.9 collective-permute-start.30
  709.7 8.9 collective-permute-start.24
  709.7 8.9 collective-permute-start.31
  718.6 9.3 collective-permute-start.25
  718.6 9.3 collective-permute-start.32
  727.9 10.5 collective-permute-start.26
  727.9 10.9 collective-permute-start.33
  743.6 68.6 %copy-start.6 = (bf16[96,1536]{1,0:T(8,128)(2,1)S(1)}, bf16[96,1536]{1,0:T(8,128)(2,1)}, u32[]{:S(2)}) copy-start(bf16[96,1536]{1,0:T(8,128)(2,1)} %fusion.19) | copy-start | bytes 884740
  743.6 129.6 %all-gather.35.cloned.1.call-start = ((), (), s32[]{:S(2)}) async-start(), calls=%async_computation.8 | async-start | bytes 5013504 | tf_op jit(solution)/shard_map/all_gather | solution.py:45
  746.9 130.2 %copy-start.1 = (bf16[96,1536]{1,0:T(8,128)(2,1)}, bf16[96,1536]{1,0:T(8,128)(2,1)S(1)}, u32[]{:S(2)}) copy-start(bf16[96,1536]{1,0:T(8,128)(2,1)S(1)} %fusion.36) | copy-start | bytes 884740
  747.0 6.8 collective-permute-start.34
  754.5 179.6 %all-gather.39.cloned.1.call-start = ((), (), s32[]{:S(2)}) async-start(), calls=%async_computation.10 | async-start | bytes 5013504 | tf_op jit(solution)/shard_map/all_gather | solution.py:46
  755.1 240.6 %all-gather.37.cloned.1.call-start = ((), (), s32[]{:S(2)}) async-start(), calls=%async_computation.9 | async-start | bytes 5013504 | tf_op jit(solution)/shard_map/all_gather | solution.py:61
  815.5 180.2 %copy-start = (bf16[96,1536]{1,0:T(8,128)(2,1)S(1)}, bf16[96,1536]{1,0:T(8,128)(2,1)}, u32[]{:S(2)}) copy-start(bf16[96,1536]{1,0:T(8,128)(2,1)} %fusion.31) | copy-start | bytes 884740
  877.2 179.4 %all-gather.43.cloned.1.call-start = ((), (), s32[]{:S(2)}) async-start(), calls=%async_computation.12 | async-start | bytes 5013504 | tf_op jit(solution)/shard_map/all_gather | solution.py:49
  877.8 125.1 %copy-start.2 = (bf16[96,1536]{1,0:T(8,128)(2,1)S(1)}, bf16[96,1536]{1,0:T(8,128)(2,1)}, u32[]{:S(2)}) copy-start(bf16[96,1536]{1,0:T(8,128)(2,1)} %copy-done.1) | copy-start | bytes 884740
  877.8 239.6 %all-gather.41.cloned.1.call-start = ((), (), s32[]{:S(2)}) async-start(), calls=%async_computation.11 | async-start | bytes 5013504 | tf_op jit(solution)/shard_map/all_gather | solution.py:66
  938.1 240.8 %all-gather.45.cloned.1.call-start = ((), (), s32[]{:S(2)}) async-start(), calls=%async_computation.13 | async-start | bytes 5013504 | tf_op jit(solution)/shard_map/all_gather | solution.py:74
  999.7 127.1 %collective-permute-start.35 = (bf16[96,1536]{1,0:T(8,128)(2,1)S(1)}, bf16[96,1536]{1,0:T(8,128)(2,1)S(1)}, u32[]{:S(2)}, u32[]{:S(2)}) collective-permute-start(bf16[96,1536]{1,0:T(8,128)(2,1)S(1)} %copy-done), channel_id=1, source_target_pairs={{0,32},{16,48},{32,64},{48,80},{64,96},{80,112},{96,128},{112,144}... | collective-permute-start | bytes 884744 | tf_op jit(solution)/shard_map/ppermute | solution.py:26
  (1 other events, 0.7 us)
Sparse Core Ops, SparseCore 0:
  10.4 62.4 all-gather.46
  163.5 63.5 all-gather.18
  230.1 58.5 all-gather.20
  292.8 58.5 all-gather.22
  353.6 58.5 all-gather.24
  415.1 58.5 all-gather.28
  476.1 58.5 all-gather.48
  537.7 58.5 all-gather.26
  599.3 58.5 all-gather.30
  743.8 68.4 all-gather.32
  814.7 58.5 all-gather.34
  875.5 58.5 all-gather.38
  937.1 58.5 all-gather.36
  998.0 58.5 all-gather.42
  1058.8 58.5 all-gather.40
  1120.3 58.5 all-gather.44
